TPU v7x, 32 devices: a whole 2x2x4 slice. The times are simulated.
32 devices in a mesh: body: 4 (over z), mort: 8 (over y, x, core).
Axes of the slice: x: 2, y: 2, z: 4, core: 2. Of those that a mesh axis runs over, the one named last changes fastest.
Arguments:
- displacement: float32 [3, 64, 256, 128], P(None, 'body', 'mort'), may hold values from -6 to 6
- body_load: float32 [3, 64, 256, 128], P(None, 'body', 'mort'), may hold values from -6 to 6
- stiffness: float32 [64, 256, 128], P('body', 'mort'), may hold values from 0.5 to 4
- initial_gap: float32 [4096, 128], P(('body', 'mort')), may hold values from -6 to 6
- weights: float32 [4096, 128], P(('body', 'mort')), may hold values from 0.05 to 1
- basis_values: float32 [4096, 4, 128], P(('body', 'mort')), may hold values from 0 to 1
- point_cell: int32 [4096, 128], P(('body', 'mort')), may hold values from 0 to 511
- point_segment: int32 [4096, 128], P(('body', 'mort')), may hold values from 0 to 255
- block_owner: int32 [4096, 1], P(('body', 'mort')), may hold values from 0 to 7; in each aligned block of 128 rows (0 to 127, 128 to 255, ...) at most 64 rows name the same one
- multipliers: float32 [4, 8192], P(None, ('body', 'mort')), may hold values from 0 to 2
- block_inverse: float32 [4, 4, 8192], P(None, None, ('body', 'mort')), may hold values from -0.9 to 1
Outputs:
- body_residual: float32 [3, 64, 256, 128], P(None, 'body', 'mort')
- new_multipliers: float32 [4, 8192], P(None, ('body', 'mort'))
Inputs may be any that keep to these rules, and one draw needn't show every extreme that they name: `block_owner`: among the 128 blocks of one device each owner is named at most 64 times.
All inputs are finite; a program needn't handle non-finite values.
Results may differ from a plain program's by a relative error of at most 0.000098.
Values sent between devices are 32-bit elements; how exact they have to be, the bound alone decides.
A program may use at most 128 MiB of HBM per device.

v0:
```python
import math
import jax
import jax.numpy as jnp
from jax import lax
from jax.sharding import PartitionSpec as P

exact = lax.Precision.HIGHEST


def extended(block, sides, width):
    for axis, dim in sides:
        count = lax.axis_size(axis)
        forward = [(i, i + 1) for i in range(count - 1)]
        backward = [(target, source) for source, target in forward]
        low = lax.ppermute(
            lax.slice_in_dim(block, block.shape[dim] - width, None, axis=dim), axis, forward
        )
        high = lax.ppermute(lax.slice_in_dim(block, 0, width, axis=dim), axis, backward)
        block = jnp.concatenate([low, block, high], axis=dim)
    return block


def grouped(fn, arrays, group):
    count = arrays[0].shape[0]
    shaped = tuple((a.reshape((count // group, group) + a.shape[1:]) for a in arrays))
    return lax.map(lambda items: fn(*items), shaped)


def newton_update(integrals, multipliers, block_inverse):
    applied = jnp.sum(block_inverse * integrals[None, :, :], axis=1)
    updated = jnp.maximum(multipliers - applied, 0.0)
    return (updated, updated - multipliers)


def body(
    displacement,
    body_load,
    stiffness,
    initial_gap,
    weights,
    basis_values,
    point_cell,
    point_segment,
    block_owner,
    multipliers,
    block_inverse,
):
    cells_x = displacement.shape[1]
    cells_y = displacement.shape[2]
    blocks = initial_gap.shape[0]
    points = initial_gap.shape[1]
    segments = multipliers.shape[1]
    mort_count = lax.axis_size("mort")
    group = math.gcd(blocks, 16)
    cell_ids = jnp.arange(cells_x * cells_y, dtype=jnp.int32)
    segment_ids_all = jnp.arange(segments, dtype=jnp.int32)
    surface = displacement[2, :, :, 0].reshape(cells_x * cells_y)

    def lookup(cells):
        onehot = (cells[:, :, None] == cell_ids[None, None, :]).astype(jnp.float32)
        return jnp.einsum("gpc,c->gp", onehot, surface, precision=exact)

    point_gap = initial_gap + grouped(lookup, (point_cell,), group).reshape(blocks, points)
    integrand = weights[:, None, :] * basis_values * point_gap[:, None, :]
    owners = block_owner[:, 0]
    owner_onehot = (owners[:, None] == jnp.arange(mort_count, dtype=jnp.int32)[None, :]).astype(
        jnp.float32
    )

    def summed(segs, terms, owner_rows):
        onehot = (segs[:, :, None] == segment_ids_all[None, None, :]).astype(jnp.float32)
        return jnp.einsum("gps,gkp,go->oks", onehot, terms, owner_rows, precision=exact)

    partial_value = jnp.sum(
        grouped(summed, (point_segment, integrand, owner_onehot), group), axis=0
    )
    integrals = lax.psum_scatter(partial_value, "mort", scatter_dimension=0, tiled=True)[0]
    updated, change = newton_update(integrals, multipliers, block_inverse)
    changes = lax.all_gather(change[None], "mort", axis=0, tiled=True)
    block_changes = jnp.einsum("bo,oks->bks", owner_onehot, changes, precision=exact)

    def picked(segs, basis, table):
        onehot = (segs[:, :, None] == segment_ids_all[None, None, :]).astype(jnp.float32)
        return jnp.einsum("gps,gks,gkp->gp", onehot, table, basis, precision=exact)

    pressure = grouped(picked, (point_segment, basis_values, block_changes), group).reshape(
        blocks, points
    )

    def spread(cells, loads):
        onehot = (cells[:, :, None] == cell_ids[None, None, :]).astype(jnp.float32)
        return jnp.einsum("gpc,gp->c", onehot, loads, precision=exact)

    traction = jnp.sum(grouped(spread, (point_cell, weights * pressure), group), axis=0)
    padded = extended(displacement, (("body", 1), ("mort", 2)), 1)
    padded = jnp.pad(padded, ((0, 0), (0, 0), (0, 0), (1, 1)))
    beside = padded[:, 2:, 1:-1, 1:-1] + padded[:, :-2, 1:-1, 1:-1]
    beside = beside + padded[:, 1:-1, 2:, 1:-1] + padded[:, 1:-1, :-2, 1:-1]
    beside = beside + padded[:, 1:-1, 1:-1, 2:] + padded[:, 1:-1, 1:-1, :-2]
    stiff_force = (6.0 + stiffness)[None] * displacement - beside
    residual = body_load - stiff_force
    residual = residual.at[2, :, :, 0].add(traction.reshape(cells_x, cells_y))
    return (residual, updated)


def solution(mesh):
    return jax.shard_map(
        body,
        mesh=mesh,
        in_specs=(
            P(None, "body", "mort", None),
            P(None, "body", "mort", None),
            P("body", "mort", None),
            P(("body", "mort"), None),
            P(("body", "mort"), None),
            P(("body", "mort"), None, None),
            P(("body", "mort"), None),
            P(("body", "mort"), None),
            P(("body", "mort"), None),
            P(None, ("body", "mort")),
            P(None, None, ("body", "mort")),
        ),
        out_specs=(P(None, "body", "mort", None), P(None, ("body", "mort"))),
        check_vma=False,
    )
```

profile of v0, /device:TPU:19, one launch (start us, length us, event | category | flops | bytes accessed | tf_op | source)
XLA Modules:
  0.0 152.1 jit_solution(2052006497745772095)
XLA Ops:
  1.5 3.3 %collective-permute-start.1 = (f32[3,1,32,128]{3,2,1,0:T(8,128)S(1)}, f32[3,1,32,128]{3,2,1,0:T(8,128)S(1)}, u32[]{:S(2)}, u32[]{:S(2)}) collective-permute-start(f32[3,1,32,128]{3,2,1,0:T(8,128)S(1)} %get-tuple-element.245), channel_id=1, source_target_pairs={{0,8},{8,16},{16,24},{1,9},{9,17},{17,25},{2,10},{10,18},{18,26},{... | collective-permute-start | bytes 147464 | tf_op jit(solution)/shard_map/ppermute | solution.py:15
  4.9 2.1 %collective-permute-start = (f32[3,1,32,128]{3,2,1,0:T(8,128)S(1)}, f32[3,1,32,128]{3,2,1,0:T(8,128)S(1)}, u32[]{:S(2)}, u32[]{:S(2)}) collective-permute-start(f32[3,1,32,128]{3,2,1,0:T(8,128)S(1)} %get-tuple-element.244), channel_id=1, source_target_pairs={{8,0},{16,8},{24,16},{9,1},{17,9},{25,17},{10,2},{18,10},{26,18},{... | collective-permute-start | bytes 147464 | tf_op jit(solution)/shard_map/ppermute | solution.py:18
  8.2 21.5 %while.45 = (s32[]{:T(128)}, f32[8,16,128]{2,1,0:T(8,128)S(1)}, s32[8,16,128]{2,1,0:T(8,128)}, f32[512]{0:T(512)S(1)}, s32[]{:T(128)}) while((s32[]{:T(128)}, f32[8,16,128]{2,1,0:T(8,128)S(1)}, s32[8,16,128]{2,1,0:T(8,128)}, f32[512]{0:T(512)S(1)}, s32[]{:T(128)}) %tuple.106), condition=%wide.region_1.2_spmd.clone, body=%wide.region_0.1_spmd.clone.sunk | while | flops 13631490 | bytes 51269 | solution.py:26
  8.9 2.0 %fusion.54 = f32[1,16,128]{2,0,1:T(1,128)S(1)} fusion(f32[512,1,1]{0,1,2:T(1,128)S(1)} %bitcast.110, s32[16,128]{1,0:T(8,128)S(1)} %dynamic-slice_bitcast_fusion.9), kind=kOutput, calls=%fused_computation.5.clone.1 | convolution fusion | flops 13631488 | bytes 18432 | tf_op jit(solution)/shard_map/while/body/eval_jaxpr/gpc,c->gp/dot_general | solution.py:61
  11.6 2.0 %fusion.54 = f32[1,16,128]{2,0,1:T(1,128)S(1)} fusion(f32[512,1,1]{0,1,2:T(1,128)S(1)} %bitcast.110, s32[16,128]{1,0:T(8,128)S(1)} %dynamic-slice_bitcast_fusion.9), kind=kOutput, calls=%fused_computation.5.clone.1 | convolution fusion | flops 13631488 | bytes 18432 | tf_op jit(solution)/shard_map/while/body/eval_jaxpr/gpc,c->gp/dot_general | solution.py:61
  14.3 2.0 %fusion.54 = f32[1,16,128]{2,0,1:T(1,128)S(1)} fusion(f32[512,1,1]{0,1,2:T(1,128)S(1)} %bitcast.110, s32[16,128]{1,0:T(8,128)S(1)} %dynamic-slice_bitcast_fusion.9), kind=kOutput, calls=%fused_computation.5.clone.1 | convolution fusion | flops 13631488 | bytes 18432 | tf_op jit(solution)/shard_map/while/body/eval_jaxpr/gpc,c->gp/dot_general | solution.py:61
  17.0 2.0 %fusion.54 = f32[1,16,128]{2,0,1:T(1,128)S(1)} fusion(f32[512,1,1]{0,1,2:T(1,128)S(1)} %bitcast.110, s32[16,128]{1,0:T(8,128)S(1)} %dynamic-slice_bitcast_fusion.9), kind=kOutput, calls=%fused_computation.5.clone.1 | convolution fusion | flops 13631488 | bytes 18432 | tf_op jit(solution)/shard_map/while/body/eval_jaxpr/gpc,c->gp/dot_general | solution.py:61
  19.6 2.0 %fusion.54 = f32[1,16,128]{2,0,1:T(1,128)S(1)} fusion(f32[512,1,1]{0,1,2:T(1,128)S(1)} %bitcast.110, s32[16,128]{1,0:T(8,128)S(1)} %dynamic-slice_bitcast_fusion.9), kind=kOutput, calls=%fused_computation.5.clone.1 | convolution fusion | flops 13631488 | bytes 18432 | tf_op jit(solution)/shard_map/while/body/eval_jaxpr/gpc,c->gp/dot_general | solution.py:61
  22.3 2.0 %fusion.54 = f32[1,16,128]{2,0,1:T(1,128)S(1)} fusion(f32[512,1,1]{0,1,2:T(1,128)S(1)} %bitcast.110, s32[16,128]{1,0:T(8,128)S(1)} %dynamic-slice_bitcast_fusion.9), kind=kOutput, calls=%fused_computation.5.clone.1 | convolution fusion | flops 13631488 | bytes 18432 | tf_op jit(solution)/shard_map/while/body/eval_jaxpr/gpc,c->gp/dot_general | solution.py:61
  25.0 2.0 %fusion.54 = f32[1,16,128]{2,0,1:T(1,128)S(1)} fusion(f32[512,1,1]{0,1,2:T(1,128)S(1)} %bitcast.110, s32[16,128]{1,0:T(8,128)S(1)} %dynamic-slice_bitcast_fusion.9), kind=kOutput, calls=%fused_computation.5.clone.1 | convolution fusion | flops 13631488 | bytes 18432 | tf_op jit(solution)/shard_map/while/body/eval_jaxpr/gpc,c->gp/dot_general | solution.py:61
  27.7 2.0 %fusion.54 = f32[1,16,128]{2,0,1:T(1,128)S(1)} fusion(f32[512,1,1]{0,1,2:T(1,128)S(1)} %bitcast.110, s32[16,128]{1,0:T(8,128)S(1)} %dynamic-slice_bitcast_fusion.9), kind=kOutput, calls=%fused_computation.5.clone.1 | convolution fusion | flops 13631488 | bytes 18432 | tf_op jit(solution)/shard_map/while/body/eval_jaxpr/gpc,c->gp/dot_general | solution.py:61
  31.1 13.5 %while.46 = (s32[]{:T(128)}, f32[8,8,4,256]{3,1,2,0:T(8,128)S(1)}, f32[8,16,8]{1,2,0:T(8,128)S(1)}, f32[8,16,4,128]{3,2,1,0:T(4,128)S(1)}, s32[8,16,128]{2,1,0:T(8,128)}, /*index=5*/s32[]{:T(128)}) while((s32[]{:T(128)}, f32[8,8,4,256]{3,1,2,0:T(8,128)S(1)}, f32[8,16,8]{1,2,0:T(8,128)S(1)}, f32[8,16,4,128]{3,2,1,0:T(4,128)S(1)}, ...), condition=%wide.region_3.4_spmd.clone, body=%wide.region_2.3_spmd.clone.sunk | while | flops 27262976 | bytes 226381 | solution.py:26
  44.7 21.7 %all-reduce.1 = f32[8,4,256]{2,1,0:T(4,128)S(1)} all-reduce(f32[8,4,256]{2,1,0:T(4,128)S(1)} %copy.33), channel_id=3, replica_groups=mesh['body'=4,'mort'=8] {'mort'}, use_global_device_ids=true, to_apply=%region_5.6.clone | all-reduce | flops 8192 | bytes 65536
  68.2 11.0 %all-gather.1 = f32[8,4,256]{2,1,0:T(4,128)S(1)} all-gather(f32[1,4,256]{2,1,0:T(4,128)S(1)} %get-tuple-element.235), channel_id=2, replica_groups=mesh['body'=4,'mort'=8] {'mort'}, dimensions={0}, use_global_device_ids=true | all-gather | bytes 36864 | tf_op jit(solution)/shard_map/all_gather | solution.py:79
  79.7 14.8 %while.47 = (s32[]{:T(128)}, f32[8,16,128]{2,1,0:T(8,128)S(1)}, f32[8,16,4,128]{3,2,1,0:T(4,128)S(1)}, f32[8,16,4,256]{3,1,0,2:T(8,128)S(1)}, s32[8,16,128]{2,1,0:T(8,128)}, /*index=5*/s32[]{:T(128)}) while((s32[]{:T(128)}, f32[8,16,128]{2,1,0:T(8,128)S(1)}, f32[8,16,4,128]{3,2,1,0:T(4,128)S(1)}, f32[8,16,4,256]{3,1,0,2:T(8,128)S(1)}, ...), condition=%wide.region_8.9_spmd.clone, body=%wide.region_7.8_spmd.clone.sunk | while | flops 25704448 | bytes 278613 | solution.py:26
  94.6 17.8 %while.48 = (s32[]{:T(128)}, f32[8,512]{1,0:T(8,128)S(1)}, s32[8,16,128]{2,1,0:T(8,128)}, f32[8,16,128]{2,1,0:T(8,128)S(1)}, s32[]{:T(128)}, /*index=5*/s32[]{:T(128)}) while((s32[]{:T(128)}, f32[8,512]{1,0:T(8,128)S(1)}, s32[8,16,128]{2,1,0:T(8,128)}, f32[8,16,128]{2,1,0:T(8,128)S(1)}, s32[]{:T(128)}, ...), condition=%wide.region_10.11_spmd.clone, body=%wide.region_9.10_spmd.clone.sunk | while | flops 13631490 | bytes 55377 | solution.py:26
  95.4 1.4 fusion.62
  97.6 1.4 fusion.62
  99.8 1.4 fusion.62
  108.7 1.4 fusion.62
  110.9 1.4 fusion.62
  113.6 2.1 %collective-permute-start.2 = (f32[3,18,1,128]{3,2,1,0:T(1,128)S(1)}, f32[3,18,1,128]{3,2,1,0:T(1,128)S(1)}, u32[]{:S(2)}, u32[]{:S(2)}) collective-permute-start(f32[3,18,1,128]{3,2,1,0:T(1,128)S(1)} %get-tuple-element.240), channel_id=1, source_target_pairs={{1,0},{2,1},{3,2},{4,3},{5,4},{6,5},{7,6},{9,8},{10,9},{11,10},{12... | collective-permute-start | bytes 82952 | tf_op jit(solution)/shard_map/ppermute | solution.py:18
  115.7 4.4 %collective-permute-start.3 = (f32[3,18,1,128]{3,2,1,0:T(1,128)S(1)}, f32[3,18,1,128]{3,2,1,0:T(1,128)S(1)}, u32[]{:S(2)}, u32[]{:S(2)}) collective-permute-start(f32[3,18,1,128]{3,2,1,0:T(1,128)S(1)} %get-tuple-element.239), channel_id=1, source_target_pairs={{0,1},{1,2},{2,3},{3,4},{4,5},{5,6},{6,7},{8,9},{9,10},{10,11},{11... | collective-permute-start | bytes 82952 | tf_op jit(solution)/shard_map/ppermute | solution.py:15
  120.1 2.2 %copy.26 = f32[3,16,32,128]{2,1,3,0:T(8,128)} copy(f32[3,16,32,128]{3,2,1,0:T(8,128)S(1)} %copy-done) | data formatting | bytes 1572864 | tf_op args[0]
  122.4 3.2 %copy.32 = f32[3,16,32,128]{2,1,3,0:T(8,128)} copy(f32[3,16,32,128]{3,2,1,0:T(8,128)} %param.22) | data formatting | bytes 1572864 | tf_op args[1]
  127.0 2.2 %copy.46 = f32[3,16,32,128]{2,1,3,0:T(8,128)} copy(f32[3,16,32,128]{3,2,1,0:T(8,128)S(1)} %copy-done.1) | data formatting | bytes 1572864
  129.3 2.2 %copy.47 = f32[3,16,32,128]{2,1,3,0:T(8,128)} copy(f32[3,16,32,128]{3,2,1,0:T(8,128)S(1)} %get-tuple-element.241) | data formatting | bytes 1572864
  131.7 2.3 %copy.48 = f32[3,16,32,128]{2,1,3,0:T(8,128)} copy(f32[3,16,32,128]{3,2,1,0:T(8,128)S(1)} %get-tuple-element.237) | data formatting | bytes 1572864
  134.0 2.3 %copy.49 = f32[3,16,32,128]{2,1,3,0:T(8,128)} copy(f32[3,16,32,128]{3,2,1,0:T(8,128)S(1)} %get-tuple-element.238) | data formatting | bytes 1572864
  136.4 3.4 %copy.31 = f32[3,18,34,128]{2,1,3,0:T(8,128)} copy(f32[3,18,34,128]{3,2,1,0:T(8,128)S(1)} %pad_maximum_fusion) | data formatting | bytes 1880064 | tf_op jit(solution)/shard_map/concatenate | solution.py:19
  139.8 10.4 %fusion.31 = f32[3,16,32,128]{2,1,3,0:T(8,128)S(1)} fusion(f32[3,16,32,128]{2,1,3,0:T(8,128)} %copy.32, f32[3,18,34,128]{2,1,3,0:T(8,128)} %copy.31, f32[3,16,32,128]{2,1,3,0:T(8,128)} %copy.49, f32[3,16,32,128]{2,1,3,0:T(8,128)} %copy.48, f32[3,16,32,128]{2,1,3,0:T(8,128)} %copy.46, f32[3,16,32,128]{2,1,3,0:T(8,128)} %copy.47, f32[3,16,32,128]{2,1,3,0:T(8,128)} %copy.26, ...), kind=kLoop, calls=%fused_computation.43 | loop fusion | flops 1572864 | bytes 6707200 | tf_op jit(solution)/shard_map/sub | solution.py:101
  150.3 1.9 %copy.36 = f32[3,16,32,128]{3,2,1,0:T(8,128)} copy(f32[3,16,32,128]{2,1,3,0:T(8,128)S(1)} %fusion.35) | data formatting | bytes 1572864
  (155 shorter events, 52.7 us)
Async XLA Ops:
  0.6 29.6 %copy-start.8 = (s32[128,1]{0,1:T(1,128)S(1)}, s32[128,1]{0,1:T(1,128)}, u32[]{:S(2)}) copy-start(s32[128,1]{0,1:T(1,128)} %param.29) | copy-start | bytes 1540
  0.6 30.4 %copy-start.5 = (f32[128,128]{1,0:T(8,128)S(1)}, f32[128,128]{1,0:T(8,128)}, u32[]{:S(2)}) copy-start(f32[128,128]{1,0:T(8,128)} %param.24) | copy-start | bytes 196612
  1.5 29.5 %copy-start.2 = (f32[128,128]{1,0:T(8,128)S(1)}, f32[128,128]{1,0:T(8,128)}, u32[]{:S(2)}) copy-start(f32[128,128]{1,0:T(8,128)} %param.25) | copy-start | bytes 196612
  1.5 29.5 %copy-start.3 = (f32[128,4,128]{2,1,0:T(4,128)S(1)}, f32[128,4,128]{2,1,0:T(4,128)}, u32[]{:S(2)}) copy-start(f32[128,4,128]{2,1,0:T(4,128)} %param.26) | copy-start | bytes 786436
  1.5 110.9 %collective-permute-start.1 = (f32[3,1,32,128]{3,2,1,0:T(8,128)S(1)}, f32[3,1,32,128]{3,2,1,0:T(8,128)S(1)}, u32[]{:S(2)}, u32[]{:S(2)}) collective-permute-start(f32[3,1,32,128]{3,2,1,0:T(8,128)S(1)} %get-tuple-element.245), channel_id=1, source_target_pairs={{0,8},{8,16},{16,24},{1,9},{9,17},{17,25},{2,10},{10,18},{18,26},{... | collective-permute-start | bytes 147464 | tf_op jit(solution)/shard_map/ppermute | solution.py:15
  4.9 107.6 %collective-permute-start = (f32[3,1,32,128]{3,2,1,0:T(8,128)S(1)}, f32[3,1,32,128]{3,2,1,0:T(8,128)S(1)}, u32[]{:S(2)}, u32[]{:S(2)}) collective-permute-start(f32[3,1,32,128]{3,2,1,0:T(8,128)S(1)} %get-tuple-element.244), channel_id=1, source_target_pairs={{8,0},{16,8},{24,16},{9,1},{17,9},{25,17},{10,2},{18,10},{26,18},{... | collective-permute-start | bytes 147464 | tf_op jit(solution)/shard_map/ppermute | solution.py:18
  29.7 36.7 %copy-start.9 = (u32[32]{0:T(128)S(1)}, u32[32]{0:T(128)}, u32[]{:S(2)}) copy-start(u32[32]{0:T(128)} %constant.89) | copy-start | bytes 388
  29.7 37.9 %copy-start.6 = (f32[4,4,256]{2,1,0:T(4,128)S(1)}, f32[4,4,256]{2,1,0:T(4,128)}, u32[]{:S(2)}) copy-start(f32[4,4,256]{2,1,0:T(4,128)} %param.31) | copy-start | bytes 49156
  29.7 37.9 %copy-start.7 = (f32[4,256]{1,0:T(4,128)S(1)}, f32[4,256]{1,0:T(4,128)}, u32[]{:S(2)}) copy-start(f32[4,256]{1,0:T(4,128)} %param.30) | copy-start | bytes 12292
  94.6 17.9 %copy-start = (f32[3,16,32,128]{3,2,1,0:T(8,128)S(1)}, f32[3,16,32,128]{3,2,1,0:T(8,128)}, u32[]{:S(2)}) copy-start(f32[3,16,32,128]{3,2,1,0:T(8,128)} %param.21) | copy-start | bytes 2359300
  112.4 7.7 %copy-start.4 = (f32[16,32,128]{2,1,0:T(8,128)S(1)}, f32[16,32,128]{2,1,0:T(8,128)}, u32[]{:S(2)}) copy-start(f32[16,32,128]{2,1,0:T(8,128)} %param.23) | copy-start | bytes 786436
  113.6 17.9 %collective-permute-start.2 = (f32[3,18,1,128]{3,2,1,0:T(1,128)S(1)}, f32[3,18,1,128]{3,2,1,0:T(1,128)S(1)}, u32[]{:S(2)}, u32[]{:S(2)}) collective-permute-start(f32[3,18,1,128]{3,2,1,0:T(1,128)S(1)} %get-tuple-element.240), channel_id=1, source_target_pairs={{1,0},{2,1},{3,2},{4,3},{5,4},{6,5},{7,6},{9,8},{10,9},{11,10},{12... | collective-permute-start | bytes 82952 | tf_op jit(solution)/shard_map/ppermute | solution.py:18
  115.7 15.8 %collective-permute-start.3 = (f32[3,18,1,128]{3,2,1,0:T(1,128)S(1)}, f32[3,18,1,128]{3,2,1,0:T(1,128)S(1)}, u32[]{:S(2)}, u32[]{:S(2)}) collective-permute-start(f32[3,18,1,128]{3,2,1,0:T(1,128)S(1)} %get-tuple-element.239), channel_id=1, source_target_pairs={{0,1},{1,2},{2,3},{3,4},{4,5},{5,6},{6,7},{8,9},{9,10},{10,11},{11... | collective-permute-start | bytes 82952 | tf_op jit(solution)/shard_map/ppermute | solution.py:15
  122.4 4.7 %copy-start.1 = (f32[3,16,32,128]{3,2,1,0:T(8,128)S(1)}, f32[3,16,32,128]{3,2,1,0:T(8,128)}, u32[]{:S(2)}) copy-start(f32[3,16,32,128]{3,2,1,0:T(8,128)} %get-tuple-element.242) | copy-start | bytes 2359300
where the time goes:
time: 154 us; the launch traced here: 152 us
  local copies, waits for them, and re-layouts  48.4 us (31%)
  matrix products  44.1 us (29%)
  blocking collectives  32.7 us (21%)
  other arithmetic  13.4 us (9%)
  starting transfers between devices  11.9 us (8%)
    unnamed x1, blocking collectives  21.7 us
    unnamed x30, local copies, waits for them, and re-layouts  17.5 us
    dot_general x8, matrix products, lookup(): return jnp.einsum('gpc,c->gp', onehot, surface, precision=exact)  15.8 us
    dot_general x8, matrix products, spread(): return jnp.einsum('gpc,gp->c', onehot, loads, precision=exact)  11.5 us
    all_gather x1, blocking collectives, body(): changes = lax.all_gather(change[None], 'mort', axis=0, tiled=True)  11 us
    sub x1, other arithmetic, body(): residual = body_load - stiff_force  10.4 us
    dot_general x8, matrix products, picked(): return jnp.einsum('gps,gks,gkp->gp', onehot, table, basis, precision=exact)  8.74 us
    ppermute x2, starting transfers between devices, extended(): lax.ppermute(lax.slice_in_dim(block, block.shape[dim] - width, None, axis...  7.73 us
  transfers between devices with their start and end apart: 4, of which 0 were waited for; matrix products, arithmetic and copies ran while one was open for 55% of the time, Pallas kernels for 0%

commit v1 on v0

--- a/solution.py
+++ b/solution.py
@@ -76,7 +76,9 @@
     )
     integrals = lax.psum_scatter(partial_value, "mort", scatter_dimension=0, tiled=True)[0]
     updated, change = newton_update(integrals, multipliers, block_inverse)
-    changes = lax.all_gather(change[None], "mort", axis=0, tiled=True)
+    changes = jnp.concatenate(
+        lax.all_to_all(jnp.stack([change[None]] * lax.axis_size("mort")), "mort", 0, 0), axis=0
+    )
     block_changes = jnp.einsum("bo,oks->bks", owner_onehot, changes, precision=exact)
 
     def picked(segs, basis, table):

time: 154 us -> 150 us (0.974)
  blocking collectives: 32.7 us -> 21.8 us
  starting transfers between devices: 11.9 us -> 18.5 us
    all_gather x1 -> x0, blocking collectives: 11 us -> none  [body(): changes = lax.all_gather(change[None], 'mort', axis=0, tiled=True)]
    all_to_all x0 -> x1, starting transfers between devices: none -> 6.49 us  [body(): lax.all_to_all(jnp.stack([change[None]] * lax.axis_size('mort')), 'mort',...]
    unnamed x30 -> x32, local copies, waits for them, and re-layouts: 17.5 us -> 16.5 us
  transfers between devices with their start and end apart: 4 -> 5, of which waited for: 0 -> 0; matrix products, arithmetic and copies ran while one was open for 55% -> 56% of each run, Pallas kernels for 0% -> 0%
where the time goes in v1:
time: 150 us; the launch traced here: 147 us
  local copies, waits for them, and re-layouts  48 us (32%)
  matrix products  44.1 us (29%)
  blocking collectives  21.8 us (15%)
  starting transfers between devices  18.5 us (12%)
  other arithmetic  13.4 us (9%)
    unnamed x1, blocking collectives  21.8 us
    unnamed x32, local copies, waits for them, and re-layouts  16.5 us
    dot_general x8, matrix products, lookup(): return jnp.einsum('gpc,c->gp', onehot, surface, precision=exact)  15.8 us
    dot_general x8, matrix products, spread(): return jnp.einsum('gpc,gp->c', onehot, loads, precision=exact)  11.5 us
    sub x1, other arithmetic, body(): residual = body_load - stiff_force  10.4 us
    dot_general x8, matrix products, picked(): return jnp.einsum('gps,gks,gkp->gp', onehot, table, basis, precision=exact)  8.74 us
    dot_general x16, matrix products, summed(): jnp.einsum('gps,gkp,go->oks', onehot, terms, owner_rows, precision=exact)  7.7 us
    ppermute x2, starting transfers between devices, extended(): lax.ppermute(lax.slice_in_dim(block, block.shape[dim] - width, None, axis...  7.5 us
  transfers between devices with their start and end apart: 5, of which 0 were waited for; matrix products, arithmetic and copies ran while one was open for 56% of the time, Pallas kernels for 0%

profile of v1, /device:TPU:19, one launch (start us, length us, event | category | flops | bytes accessed | tf_op | source)
XLA Modules:
  0.0 147.4 jit_solution(814307359335850052)
XLA Ops:
  1.5 3.3 %collective-permute-start.1 = (f32[3,1,32,128]{3,2,1,0:T(8,128)S(1)}, f32[3,1,32,128]{3,2,1,0:T(8,128)S(1)}, u32[]{:S(2)}, u32[]{:S(2)}) collective-permute-start(f32[3,1,32,128]{3,2,1,0:T(8,128)S(1)} %get-tuple-element.245), channel_id=1, source_target_pairs={{0,8},{8,16},{16,24},{1,9},{9,17},{17,25},{2,10},{10,18},{18,26},{... | collective-permute-start | bytes 147464 | tf_op jit(solution)/shard_map/ppermute | solution.py:15
  4.9 2.1 %collective-permute-start = (f32[3,1,32,128]{3,2,1,0:T(8,128)S(1)}, f32[3,1,32,128]{3,2,1,0:T(8,128)S(1)}, u32[]{:S(2)}, u32[]{:S(2)}) collective-permute-start(f32[3,1,32,128]{3,2,1,0:T(8,128)S(1)} %get-tuple-element.244), channel_id=1, source_target_pairs={{8,0},{16,8},{24,16},{9,1},{17,9},{25,17},{10,2},{18,10},{26,18},{... | collective-permute-start | bytes 147464 | tf_op jit(solution)/shard_map/ppermute | solution.py:18
  8.2 21.5 %while.45 = (s32[]{:T(128)}, f32[8,16,128]{2,1,0:T(8,128)S(1)}, s32[8,16,128]{2,1,0:T(8,128)}, f32[512]{0:T(512)S(1)}, s32[]{:T(128)}) while((s32[]{:T(128)}, f32[8,16,128]{2,1,0:T(8,128)S(1)}, s32[8,16,128]{2,1,0:T(8,128)}, f32[512]{0:T(512)S(1)}, s32[]{:T(128)}) %tuple.105), condition=%wide.region_1.2_spmd.clone, body=%wide.region_0.1_spmd.clone.sunk | while | flops 13631490 | bytes 51269 | solution.py:26
  8.9 2.0 %fusion.56 = f32[1,16,128]{2,0,1:T(1,128)S(1)} fusion(f32[512,1,1]{0,1,2:T(1,128)S(1)} %bitcast.112, s32[16,128]{1,0:T(8,128)S(1)} %dynamic-slice_bitcast_fusion.9), kind=kOutput, calls=%fused_computation.5.clone.1 | convolution fusion | flops 13631488 | bytes 18432 | tf_op jit(solution)/shard_map/while/body/eval_jaxpr/gpc,c->gp/dot_general | solution.py:61
  11.6 2.0 %fusion.56 = f32[1,16,128]{2,0,1:T(1,128)S(1)} fusion(f32[512,1,1]{0,1,2:T(1,128)S(1)} %bitcast.112, s32[16,128]{1,0:T(8,128)S(1)} %dynamic-slice_bitcast_fusion.9), kind=kOutput, calls=%fused_computation.5.clone.1 | convolution fusion | flops 13631488 | bytes 18432 | tf_op jit(solution)/shard_map/while/body/eval_jaxpr/gpc,c->gp/dot_general | solution.py:61
  14.3 2.0 %fusion.56 = f32[1,16,128]{2,0,1:T(1,128)S(1)} fusion(f32[512,1,1]{0,1,2:T(1,128)S(1)} %bitcast.112, s32[16,128]{1,0:T(8,128)S(1)} %dynamic-slice_bitcast_fusion.9), kind=kOutput, calls=%fused_computation.5.clone.1 | convolution fusion | flops 13631488 | bytes 18432 | tf_op jit(solution)/shard_map/while/body/eval_jaxpr/gpc,c->gp/dot_general | solution.py:61
  16.9 2.0 %fusion.56 = f32[1,16,128]{2,0,1:T(1,128)S(1)} fusion(f32[512,1,1]{0,1,2:T(1,128)S(1)} %bitcast.112, s32[16,128]{1,0:T(8,128)S(1)} %dynamic-slice_bitcast_fusion.9), kind=kOutput, calls=%fused_computation.5.clone.1 | convolution fusion | flops 13631488 | bytes 18432 | tf_op jit(solution)/shard_map/while/body/eval_jaxpr/gpc,c->gp/dot_general | solution.py:61
  19.6 2.0 %fusion.56 = f32[1,16,128]{2,0,1:T(1,128)S(1)} fusion(f32[512,1,1]{0,1,2:T(1,128)S(1)} %bitcast.112, s32[16,128]{1,0:T(8,128)S(1)} %dynamic-slice_bitcast_fusion.9), kind=kOutput, calls=%fused_computation.5.clone.1 | convolution fusion | flops 13631488 | bytes 18432 | tf_op jit(solution)/shard_map/while/body/eval_jaxpr/gpc,c->gp/dot_general | solution.py:61
  22.3 2.0 %fusion.56 = f32[1,16,128]{2,0,1:T(1,128)S(1)} fusion(f32[512,1,1]{0,1,2:T(1,128)S(1)} %bitcast.112, s32[16,128]{1,0:T(8,128)S(1)} %dynamic-slice_bitcast_fusion.9), kind=kOutput, calls=%fused_computation.5.clone.1 | convolution fusion | flops 13631488 | bytes 18432 | tf_op jit(solution)/shard_map/while/body/eval_jaxpr/gpc,c->gp/dot_general | solution.py:61
  25.0 2.0 %fusion.56 = f32[1,16,128]{2,0,1:T(1,128)S(1)} fusion(f32[512,1,1]{0,1,2:T(1,128)S(1)} %bitcast.112, s32[16,128]{1,0:T(8,128)S(1)} %dynamic-slice_bitcast_fusion.9), kind=kOutput, calls=%fused_computation.5.clone.1 | convolution fusion | flops 13631488 | bytes 18432 | tf_op jit(solution)/shard_map/while/body/eval_jaxpr/gpc,c->gp/dot_general | solution.py:61
  27.7 2.0 %fusion.56 = f32[1,16,128]{2,0,1:T(1,128)S(1)} fusion(f32[512,1,1]{0,1,2:T(1,128)S(1)} %bitcast.112, s32[16,128]{1,0:T(8,128)S(1)} %dynamic-slice_bitcast_fusion.9), kind=kOutput, calls=%fused_computation.5.clone.1 | convolution fusion | flops 13631488 | bytes 18432 | tf_op jit(solution)/shard_map/while/body/eval_jaxpr/gpc,c->gp/dot_general | solution.py:61
  31.2 13.5 %while.46 = (s32[]{:T(128)}, f32[8,8,4,256]{3,1,2,0:T(8,128)S(1)}, f32[8,16,8]{1,2,0:T(8,128)S(1)}, f32[8,16,4,128]{3,2,1,0:T(4,128)S(1)}, s32[8,16,128]{2,1,0:T(8,128)}, /*index=5*/s32[]{:T(128)}) while((s32[]{:T(128)}, f32[8,8,4,256]{3,1,2,0:T(8,128)S(1)}, f32[8,16,8]{1,2,0:T(8,128)S(1)}, f32[8,16,4,128]{3,2,1,0:T(4,128)S(1)}, ...), condition=%wide.region_3.4_spmd.clone, body=%wide.region_2.3_spmd.clone.sunk | while | flops 27262976 | bytes 226381 | solution.py:26
  44.7 21.8 %all-reduce.1 = f32[8,4,256]{2,1,0:T(4,128)S(1)} all-reduce(f32[8,4,256]{2,1,0:T(4,128)S(1)} %copy.33), channel_id=2, replica_groups=mesh['body'=4,'mort'=8] {'mort'}, use_global_device_ids=true, to_apply=%region_5.6.clone | all-reduce | flops 8192 | bytes 65536
  69.0 6.5 %all-to-all-start = ((f32[8,1,4,256]{3,2,1,0:T(4,128)}), f32[8,1,4,256]{3,2,1,0:T(4,128)S(1)}, u32[]{:S(2)}, u32[]{:S(2)}) async-start(f32[8,1,4,256]{3,2,1,0:T(4,128)} %stack.3), calls=%async_computation | async-start | bytes 65536 | tf_op jit(solution)/shard_map/all_to_all | solution.py:80
  75.5 2.2 %copy.26 = f32[3,16,32,128]{2,1,3,0:T(8,128)} copy(f32[3,16,32,128]{3,2,1,0:T(8,128)S(1)} %copy-done) | data formatting | bytes 1572864 | tf_op args[0]
  77.8 2.3 %copy.32 = f32[3,16,32,128]{2,1,3,0:T(8,128)} copy(f32[3,16,32,128]{3,2,1,0:T(8,128)S(1)} %copy-done.2) | data formatting | bytes 1572864 | tf_op args[1]
  81.9 14.8 %while.47 = (s32[]{:T(128)}, f32[8,16,128]{2,1,0:T(8,128)S(1)}, f32[8,16,4,128]{3,2,1,0:T(4,128)S(1)}, f32[8,16,4,256]{3,1,2,0:T(8,128)S(1)}, s32[8,16,128]{2,1,0:T(8,128)}, /*index=5*/s32[]{:T(128)}) while((s32[]{:T(128)}, f32[8,16,128]{2,1,0:T(8,128)S(1)}, f32[8,16,4,128]{3,2,1,0:T(4,128)S(1)}, f32[8,16,4,256]{3,1,2,0:T(8,128)S(1)}, ...), condition=%wide.region_8.9_spmd.clone, body=%wide.region_7.8_spmd.clone.sunk | while | flops 25704448 | bytes 278613 | solution.py:26
  97.9 2.4 %collective-permute-start.2 = (f32[3,18,1,128]{3,2,1,0:T(1,128)S(1)}, f32[3,18,1,128]{3,2,1,0:T(1,128)S(1)}, u32[]{:S(2)}, u32[]{:S(2)}) collective-permute-start(f32[3,18,1,128]{3,2,1,0:T(1,128)S(1)} %get-tuple-element.240), channel_id=1, source_target_pairs={{1,0},{2,1},{3,2},{4,3},{5,4},{6,5},{7,6},{9,8},{10,9},{11,10},{12... | collective-permute-start | bytes 82952 | tf_op jit(solution)/shard_map/ppermute | solution.py:18
  100.3 4.2 %collective-permute-start.3 = (f32[3,18,1,128]{3,2,1,0:T(1,128)S(1)}, f32[3,18,1,128]{3,2,1,0:T(1,128)S(1)}, u32[]{:S(2)}, u32[]{:S(2)}) collective-permute-start(f32[3,18,1,128]{3,2,1,0:T(1,128)S(1)} %get-tuple-element.239), channel_id=1, source_target_pairs={{0,1},{1,2},{2,3},{3,4},{4,5},{5,6},{6,7},{8,9},{9,10},{10,11},{11... | collective-permute-start | bytes 82952 | tf_op jit(solution)/shard_map/ppermute | solution.py:15
  104.5 17.7 %while.48 = (s32[]{:T(128)}, f32[8,512]{1,0:T(8,128)S(1)}, s32[8,16,128]{2,1,0:T(8,128)}, f32[8,16,128]{2,1,0:T(8,128)S(1)}, s32[]{:T(128)}, /*index=5*/s32[]{:T(128)}) while((s32[]{:T(128)}, f32[8,512]{1,0:T(8,128)S(1)}, s32[8,16,128]{2,1,0:T(8,128)}, f32[8,16,128]{2,1,0:T(8,128)S(1)}, s32[]{:T(128)}, ...), condition=%wide.region_10.11_spmd.clone, body=%wide.region_9.10_spmd.clone.sunk | while | flops 13631490 | bytes 55377 | solution.py:26
  105.3 1.4 fusion.64
  107.5 1.4 fusion.64
  109.7 1.4 fusion.64
  111.9 1.4 fusion.64
  114.1 1.4 fusion.64
  122.4 2.2 %copy.47 = f32[3,16,32,128]{2,1,3,0:T(8,128)} copy(f32[3,16,32,128]{3,2,1,0:T(8,128)S(1)} %copy-done.1) | data formatting | bytes 1572864
  124.6 2.2 %copy.48 = f32[3,16,32,128]{2,1,3,0:T(8,128)} copy(f32[3,16,32,128]{3,2,1,0:T(8,128)S(1)} %get-tuple-element.241) | data formatting | bytes 1572864
  127.0 2.2 %copy.49 = f32[3,16,32,128]{2,1,3,0:T(8,128)} copy(f32[3,16,32,128]{3,2,1,0:T(8,128)S(1)} %get-tuple-element.237) | data formatting | bytes 1572864
  129.2 2.3 %copy.50 = f32[3,16,32,128]{2,1,3,0:T(8,128)} copy(f32[3,16,32,128]{3,2,1,0:T(8,128)S(1)} %get-tuple-element.238) | data formatting | bytes 1572864
  131.7 3.4 %copy.31 = f32[3,18,34,128]{2,1,3,0:T(8,128)} copy(f32[3,18,34,128]{3,2,1,0:T(8,128)S(1)} %pad_maximum_fusion) | data formatting | bytes 1880064 | tf_op jit(solution)/shard_map/concatenate | solution.py:19
  135.1 10.4 %fusion.31 = f32[3,16,32,128]{2,1,3,0:T(8,128)S(1)} fusion(f32[3,16,32,128]{2,1,3,0:T(8,128)} %copy.32, f32[3,18,34,128]{2,1,3,0:T(8,128)} %copy.31, f32[3,16,32,128]{2,1,3,0:T(8,128)} %copy.50, f32[3,16,32,128]{2,1,3,0:T(8,128)} %copy.49, f32[3,16,32,128]{2,1,3,0:T(8,128)} %copy.47, f32[3,16,32,128]{2,1,3,0:T(8,128)} %copy.48, f32[3,16,32,128]{2,1,3,0:T(8,128)} %copy.26, ...), kind=kLoop, calls=%fused_computation.43 | loop fusion | flops 1572864 | bytes 6707200 | tf_op jit(solution)/shard_map/sub | solution.py:103
  145.5 1.9 %copy.36 = f32[3,16,32,128]{3,2,1,0:T(8,128)} copy(f32[3,16,32,128]{2,1,3,0:T(8,128)S(1)} %fusion.39) | data formatting | bytes 1572864
  (159 shorter events, 53.3 us)
Async XLA Ops:
  0.6 29.6 %copy-start.9 = (s32[128,1]{0,1:T(1,128)S(1)}, s32[128,1]{0,1:T(1,128)}, u32[]{:S(2)}) copy-start(s32[128,1]{0,1:T(1,128)} %param.29) | copy-start | bytes 1540
  0.6 30.4 %copy-start.6 = (f32[128,128]{1,0:T(8,128)S(1)}, f32[128,128]{1,0:T(8,128)}, u32[]{:S(2)}) copy-start(f32[128,128]{1,0:T(8,128)} %param.24) | copy-start | bytes 196612
  1.5 29.5 %copy-start.3 = (f32[128,128]{1,0:T(8,128)S(1)}, f32[128,128]{1,0:T(8,128)}, u32[]{:S(2)}) copy-start(f32[128,128]{1,0:T(8,128)} %param.25) | copy-start | bytes 196612
  1.5 29.5 %copy-start.5 = (f32[128,4,128]{2,1,0:T(4,128)S(1)}, f32[128,4,128]{2,1,0:T(4,128)}, u32[]{:S(2)}) copy-start(f32[128,4,128]{2,1,0:T(4,128)} %param.26) | copy-start | bytes 786436
  1.5 95.2 %collective-permute-start.1 = (f32[3,1,32,128]{3,2,1,0:T(8,128)S(1)}, f32[3,1,32,128]{3,2,1,0:T(8,128)S(1)}, u32[]{:S(2)}, u32[]{:S(2)}) collective-permute-start(f32[3,1,32,128]{3,2,1,0:T(8,128)S(1)} %get-tuple-element.245), channel_id=1, source_target_pairs={{0,8},{8,16},{16,24},{1,9},{9,17},{17,25},{2,10},{10,18},{18,26},{... | collective-permute-start | bytes 147464 | tf_op jit(solution)/shard_map/ppermute | solution.py:15
  4.9 91.9 %collective-permute-start = (f32[3,1,32,128]{3,2,1,0:T(8,128)S(1)}, f32[3,1,32,128]{3,2,1,0:T(8,128)S(1)}, u32[]{:S(2)}, u32[]{:S(2)}) collective-permute-start(f32[3,1,32,128]{3,2,1,0:T(8,128)S(1)} %get-tuple-element.244), channel_id=1, source_target_pairs={{8,0},{16,8},{24,16},{9,1},{17,9},{25,17},{10,2},{18,10},{26,18},{... | collective-permute-start | bytes 147464 | tf_op jit(solution)/shard_map/ppermute | solution.py:18
  29.7 36.8 %copy-start.10 = (u32[32]{0:T(128)S(1)}, u32[32]{0:T(128)}, u32[]{:S(2)}) copy-start(u32[32]{0:T(128)} %constant.89) | copy-start | bytes 388
  29.7 38.1 %copy-start.7 = (f32[4,4,256]{2,1,0:T(4,128)S(1)}, f32[4,4,256]{2,1,0:T(4,128)}, u32[]{:S(2)}) copy-start(f32[4,4,256]{2,1,0:T(4,128)} %param.31) | copy-start | bytes 49156
  29.7 38.1 %copy-start.8 = (f32[4,256]{1,0:T(4,128)S(1)}, f32[4,256]{1,0:T(4,128)}, u32[]{:S(2)}) copy-start(f32[4,256]{1,0:T(4,128)} %param.30) | copy-start | bytes 12292
  29.7 45.8 %copy-start.4 = (f32[16,32,128]{2,1,0:T(8,128)S(1)}, f32[16,32,128]{2,1,0:T(8,128)}, u32[]{:S(2)}) copy-start(f32[16,32,128]{2,1,0:T(8,128)} %param.23) | copy-start | bytes 786436
  29.7 45.8 %copy-start = (f32[3,16,32,128]{3,2,1,0:T(8,128)S(1)}, f32[3,16,32,128]{3,2,1,0:T(8,128)}, u32[]{:S(2)}) copy-start(f32[3,16,32,128]{3,2,1,0:T(8,128)} %param.21) | copy-start | bytes 2359300
  44.7 33.1 %copy-start.2 = (f32[3,16,32,128]{3,2,1,0:T(8,128)S(1)}, f32[3,16,32,128]{3,2,1,0:T(8,128)}, u32[]{:S(2)}) copy-start(f32[3,16,32,128]{3,2,1,0:T(8,128)} %param.22) | copy-start | bytes 2359300
  69.0 12.4 %all-to-all-start = ((f32[8,1,4,256]{3,2,1,0:T(4,128)}), f32[8,1,4,256]{3,2,1,0:T(4,128)S(1)}, u32[]{:S(2)}, u32[]{:S(2)}) async-start(f32[8,1,4,256]{3,2,1,0:T(4,128)} %stack.3), calls=%async_computation | async-start | bytes 65536 | tf_op jit(solution)/shard_map/all_to_all | solution.py:80
  97.9 24.5 %copy-start.1 = (f32[3,16,32,128]{3,2,1,0:T(8,128)S(1)}, f32[3,16,32,128]{3,2,1,0:T(8,128)}, u32[]{:S(2)}) copy-start(f32[3,16,32,128]{3,2,1,0:T(8,128)} %get-tuple-element.242) | copy-start | bytes 2359300
  97.9 28.9 %collective-permute-start.2 = (f32[3,18,1,128]{3,2,1,0:T(1,128)S(1)}, f32[3,18,1,128]{3,2,1,0:T(1,128)S(1)}, u32[]{:S(2)}, u32[]{:S(2)}) collective-permute-start(f32[3,18,1,128]{3,2,1,0:T(1,128)S(1)} %get-tuple-element.240), channel_id=1, source_target_pairs={{1,0},{2,1},{3,2},{4,3},{5,4},{6,5},{7,6},{9,8},{10,9},{11,10},{12... | collective-permute-start | bytes 82952 | tf_op jit(solution)/shard_map/ppermute | solution.py:18
  100.3 26.5 %collective-permute-start.3 = (f32[3,18,1,128]{3,2,1,0:T(1,128)S(1)}, f32[3,18,1,128]{3,2,1,0:T(1,128)S(1)}, u32[]{:S(2)}, u32[]{:S(2)}) collective-permute-start(f32[3,18,1,128]{3,2,1,0:T(1,128)S(1)} %get-tuple-element.239), channel_id=1, source_target_pairs={{0,1},{1,2},{2,3},{3,4},{4,5},{5,6},{6,7},{8,9},{9,10},{10,11},{11... | collective-permute-start | bytes 82952 | tf_op jit(solution)/shard_map/ppermute | solution.py:15
